TPU v7x, 32 devices: a whole 2x2x4 slice. The times are simulated.
32 devices in a mesh: past: 4 (over y, x), second: 8 (over z, core).
Axes of the slice: x: 2, y: 2, z: 4, core: 2. Of those that a mesh axis runs over, the one named last changes fastest.
Arguments:
- resident: bfloat16 [12288, 12288], P('past', 'second'), may hold values from -6 to 6
- memory: bfloat16 [2, 384, 12288], P(None, None, 'past'), may hold values from -0.0546875 to 0.0546875
- previous: bfloat16 [2, 384, 12288], P(None, None, 'second'), may hold values from -6 to 6
- inverse_part: float32 [2, 384, 384], replicated, may hold values from -0.3125 to 0.3125
- pair_coupling: float32 [32, 32], replicated, may hold values from 0.0004510549 to 0.004510549
Outputs:
- fronts: bfloat16 [2, 384, 12288], P(None, None, 'second')
All inputs are finite; a program needn't handle non-finite values.
Results may differ from a plain program's by a relative error of at most 0.017.
Values may be sent and summed in bfloat16 or wider, within the bound.
A program may use at most 128 MiB of HBM per device.

v0:
```python
import jax
import jax.numpy as jnp
from jax import lax
from jax.sharding import PartitionSpec as P

step_size = 0.5


def orbital_flip(block, orbitals):
    row_count, col_count = block.shape
    blocks = block.reshape(row_count // orbitals, orbitals, col_count // orbitals, orbitals)
    return blocks.transpose(0, 3, 2, 1).reshape(row_count, col_count)


def solve_front(summed, prior, inverse_block):
    source = prior.astype(jnp.float32) - step_size * summed
    solved = source + jnp.dot(
        inverse_block, source, precision=lax.Precision.HIGHEST, preferred_element_type=jnp.float32
    )
    return solved.astype(jnp.bfloat16)


def self_energy(front, pair_coupling):
    orbitals = pair_coupling.shape[0]
    row_count, col_count = front.shape
    values = front.astype(jnp.float32)
    mirror = orbital_flip(values, orbitals)
    blocks = (values * values * mirror).reshape(
        row_count // orbitals, orbitals, col_count // orbitals, orbitals
    )
    return (
        (blocks * pair_coupling[None, :, None, :])
        .reshape(row_count, col_count)
        .astype(jnp.bfloat16)
    )


def per_device(resident, memory, previous, inverse_part, pair_coupling):
    past_count = lax.axis_size("past")

    def advance(memory_row, front_index):
        partial_value = jnp.dot(memory_row, resident, preferred_element_type=jnp.float32)
        summed = lax.psum(partial_value.astype(jnp.bfloat16), "past").astype(jnp.float32)
        prior_cols = previous[front_index]
        return solve_front(summed, prior_cols, inverse_part[front_index])

    front_one = advance(memory[0], 0)
    energy_one = self_energy(front_one, pair_coupling)
    band = energy_one.shape[0] // past_count
    own_rows = lax.dynamic_slice_in_dim(energy_one, lax.axis_index("past") * band, band, 0)
    wide_band = lax.all_gather(own_rows, "second", axis=1, tiled=True)
    gathered = lax.all_to_all(wide_band, "past", split_axis=1, concat_axis=0, tiled=True)
    orbitals = pair_coupling.shape[0]
    memory_next = (
        memory[1].astype(jnp.float32) + orbital_flip(gathered, orbitals).astype(jnp.float32)
    ).astype(jnp.bfloat16)
    front_two = advance(memory_next, 1)
    return jnp.stack([front_one, front_two])


def solution(mesh):
    in_specs = (P("past", "second"), P(None, None, "past"), P(None, None, "second"), P(), P())
    out_specs = P(None, None, "second")
    return jax.shard_map(
        per_device, mesh=mesh, in_specs=in_specs, out_specs=out_specs, check_vma=False
    )
```

profile of v0, /device:TPU:0, one launch (start us, length us, event | category | flops | bytes accessed | tf_op | source)
XLA Modules:
  0.0 301.7 jit_solution(1481439341360291000)
XLA Ops:
  6.5 9.2 %convolution_convert_fusion.1 = bf16[384,1536]{1,0:T(8,128)(2,1)} fusion(bf16[3072,1536]{1,0:T(8,128)(2,1)} %param.5, bf16[2,384,3072]{2,1,0:T(8,128)(2,1)} %param.6), kind=kOutput, calls=%fused_computation.10 | convolution fusion | flops 3624468480 | bytes 12976128 | tf_op jit(solution)/shard_map/dot_general | solution.py:42
  15.8 0.0 all-reduce.3.cloned.1.call-update
  15.8 0.0 all-gather.2.cloned.1.call-start
  15.9 4.4 %mul.29 = f32[12,32,48,32]{3,2,1,0:T(8,128)} broadcast(f32[32,32]{1,0:T(8,128)S(1)} %copy-done), dimensions={1,3} | broadcast | bytes 2363392 | tf_op jit(solution)/shard_map/mul | solution.py:32
  20.3 6.9 %mul.30 = f32[384,1536]{1,0:T(8,128)S(1)} reshape(f32[12,32,48,32]{3,2,1,0:T(8,128)} %mul.29) | data formatting | bytes 4718592 | tf_op jit(solution)/shard_map/mul | solution.py:32
  27.2 45.8 %all-reduce.3.cloned.1.call-done = bf16[384,1536]{1,0:T(8,128)(2,1)} async-done(((bf16[384,1536]{1,0:T(8,128)(2,1)}), bf16[384,1536]{1,0:T(8,128)(2,1)}) %all-reduce.3.cloned.1.call-update) | async-done | bytes 1179664 | tf_op jit(solution)/shard_map/psum | solution.py:43
  73.0 8.3 %fusion.28 = (f32[384,1536]{1,0:T(8,128)}, bf16[384,1536]{1,0:T(8,128)(2,1)S(1)}) fusion(f32[2,384,384]{2,1,0:T(8,128)} %param.8, bf16[384,1536]{1,0:T(8,128)(2,1)} %all-reduce.3.cloned.1.call-done, bf16[2,384,1536]{2,1,0:T(8,128)(2,1)} %param.7), kind=kOutput, calls=%fused_computation.40 | convolution fusion | flops 2724397056 | bytes 8847360 | tf_op jit(solution)/shard_map/dot_general | solution.py:17
  81.3 5.0 %reshape.26 = f32[12,32,48,32]{3,2,1,0:T(8,128)} reshape(bf16[384,1536]{1,0:T(8,128)(2,1)S(1)} %get-tuple-element.6) | data formatting | bytes 3538944 | tf_op jit(solution)/shard_map/reshape | solution.py:11
  86.3 10.8 %copy.8 = f32[12,32,48,32]{3,2,1,0:T(8,128)} copy(f32[12,32,48,32]{1,2,3,0:T(8,128)} %bitcast.65) | data formatting | bytes 4718592 | tf_op jit(solution)/shard_map/transpose | solution.py:12
  97.1 7.7 %reshape.27 = f32[384,1536]{1,0:T(8,128)} reshape(f32[12,32,48,32]{3,2,1,0:T(8,128)} %copy.8) | data formatting | bytes 4718592 | tf_op jit(solution)/shard_map/reshape | solution.py:12
  104.8 2.0 fusion.21
  106.9 0.0 all-gather.2.cloned.1.call-update
  106.9 0.0 all-reduce.5.cloned.1.call-start
  106.9 31.5 %all-gather.2.cloned.1.call-done = bf16[96,12288]{1,0:T(8,128)(2,1)} async-done(((bf16[96,1536]{1,0:T(8,128)(2,1)}), bf16[96,12288]{1,0:T(8,128)(2,1)}) %all-gather.2.cloned.1.call-update) | async-done | bytes 2359312 | tf_op jit(solution)/shard_map/all_gather | solution.py:51
  138.5 1.8 copy.15
  140.3 32.0 %all_to_all.13 = bf16[96,4,3072]{2,0,1:T(8,128)(2,1)S(1)} all-to-all(bf16[96,4,3072]{2,0,1:T(8,128)(2,1)S(1)} %bitcast.66), channel_id=1, replica_groups=mesh['past'=4,'second'=8] {'past'}, dimensions={1} | all-to-all | bytes 4718592 | tf_op jit(solution)/shard_map/all_to_all | solution.py:52
  172.4 2.7 convert_bitcast_fusion
  175.1 12.3 %reshape.32 = f32[12,32,96,32]{3,2,1,0:T(8,128)} reshape(f32[4,96,3072]{2,1,0:T(8,128)} %convert_bitcast_fusion) | data formatting | bytes 9437184 | tf_op jit(solution)/shard_map/convert_element_type | solution.py:55
  187.4 22.5 %copy.10 = f32[12,32,96,32]{3,2,1,0:T(8,128)} copy(f32[12,32,96,32]{1,2,3,0:T(8,128)} %bitcast.64) | data formatting | bytes 9437184 | tf_op jit(solution)/shard_map/convert_element_type | solution.py:55
  209.9 14.6 %reshape.31 = f32[384,3072]{1,0:T(8,128)} reshape(f32[12,32,96,32]{3,2,1,0:T(8,128)} %copy.10) | data formatting | bytes 9437184 | tf_op jit(solution)/shard_map/convert_element_type | solution.py:55
  224.5 10.7 %convolution_convert_fusion = bf16[384,1536]{1,0:T(8,128)(2,1)} fusion(bf16[3072,1536]{1,0:T(8,128)(2,1)} %param.5, f32[384,3072]{1,0:T(8,128)} %reshape.31, bf16[2,384,3072]{2,1,0:T(8,128)(2,1)} %param.6), kind=kOutput, calls=%fused_computation.9 | convolution fusion | flops 3628007424 | bytes 17694720 | tf_op jit(solution)/shard_map/dot_general | solution.py:42
  235.2 52.3 %all-reduce.5.cloned.1.call-done = bf16[384,1536]{1,0:T(8,128)(2,1)} async-done(((bf16[384,1536]{1,0:T(8,128)(2,1)}), bf16[384,1536]{1,0:T(8,128)(2,1)}) %all-reduce.5.cloned.1.call-update) | async-done | bytes 1179664 | tf_op jit(solution)/shard_map/psum | solution.py:43
  287.5 6.1 %fusion.5 = bf16[1,384,1536]{2,1,0:T(8,128)(2,1)S(1)} fusion(bf16[384,1536]{1,0:T(8,128)(2,1)} %all-reduce.5.cloned.1.call-done, bf16[2,384,1536]{2,1,0:T(8,128)(2,1)S(1)} %copy-done.1, f32[2,384,384]{2,1,0:T(8,128)} %param.8), kind=kOutput, calls=%fused_computation.11 | convolution fusion | flops 2723807232 | bytes 6488064 | tf_op jit(solution)/shard_map/dot_general | solution.py:17
  293.6 1.6 pad_maximum_fusion
  (6 shorter events, 0.0 us)
Async XLA Ops:
  6.5 9.3 %copy-start = (f32[32,32]{1,0:T(8,128)S(1)}, f32[32,32]{1,0:T(8,128)}, u32[]{:S(2)}) copy-start(f32[32,32]{1,0:T(8,128)} %param.9) | copy-start | bytes 12292
  6.5 66.5 %all-reduce.3.cloned.1.call-start = ((), (), s32[]{:S(2)}) async-start(), calls=%async_computation.1 | async-start | bytes 2359296 | tf_op jit(solution)/shard_map/psum | solution.py:43
  15.8 122.7 %all-gather.2.cloned.1.call-start = ((), (), s32[]{:S(2)}) async-start(), calls=%async_computation.2 | async-start | bytes 2654208 | tf_op jit(solution)/shard_map/all_gather | solution.py:51
  106.9 180.6 %all-reduce.5.cloned.1.call-start = ((), (), s32[]{:S(2)}) async-start(), calls=%async_computation.3 | async-start | bytes 2359296 | tf_op jit(solution)/shard_map/psum | solution.py:43
  224.4 63.0 %copy-start.1 = (bf16[2,384,1536]{2,1,0:T(8,128)(2,1)S(1)}, bf16[2,384,1536]{2,1,0:T(8,128)(2,1)}, u32[]{:S(2)}) copy-start(bf16[2,384,1536]{2,1,0:T(8,128)(2,1)} %param.7) | copy-start | bytes 7077892
Sparse Core Ops, SparseCore 0:
  15.9 57.0 all-reduce.2
  107.0 31.4 all-gather.1
  235.3 52.1 all-reduce.4
where the time goes:
time: 303 us; the launch traced here: 302 us
  waiting for transfers between devices  130 us (43%)
  local copies, waits for them, and re-layouts  86.1 us (28%)
  matrix products  34.3 us (11%)
  blocking collectives  32 us (11%)
  between operations  13.2 us (4%)
  other arithmetic  6.39 us (2%)
    psum x2, waiting for transfers between devices, advance(): lax.psum(partial_value.astype(jnp.bfloat16), 'past').astype(jnp.float32)  98.1 us
    convert_element_type x3, local copies, waits for them, and re-layouts, per_device(): orbital_flip(gathered, orbitals).astype(jnp.float32)  49.4 us
    all_to_all x1, blocking collectives, per_device(): lax.all_to_all(wide_band, 'past', split_axis=1, concat_axis=0, tiled=True)  32 us
    all_gather x1, waiting for transfers between devices, per_device(): wide_band = lax.all_gather(own_rows, 'second', axis=1, tiled=True)  31.5 us
    dot_general x2, matrix products, advance(): jnp.dot(memory_row, resident, preferred_element_type=jnp.float32)  19.9 us
    dot_general x2, matrix products, solve_front(): jnp.dot(inverse_block, source, precision=lax.Precision.HIGHEST, preferred...  14.3 us
    mul x2, local copies, waits for them, and re-layouts, self_energy(): blocks * pair_coupling[None, :, None, :]  11.3 us
    transpose x1, local copies, waits for them, and re-layouts, orbital_flip(): return blocks.transpose(0, 3, 2, 1).reshape(row_count, col_count)  10.8 us
  transfers between devices with their start and end apart: 3, of which 3 were waited for; matrix products, arithmetic and copies ran while one was open for 4% of the time, Pallas kernels for 0%

commit v1 on v0

--- a/solution.py
+++ b/solution.py
@@ -49,7 +49,12 @@
     band = energy_one.shape[0] // past_count
     own_rows = lax.dynamic_slice_in_dim(energy_one, lax.axis_index("past") * band, band, 0)
     wide_band = lax.all_gather(own_rows, "second", axis=1, tiled=True)
-    gathered = lax.all_to_all(wide_band, "past", split_axis=1, concat_axis=0, tiled=True)
+    gathered = jnp.concatenate(
+        lax.all_to_all(
+            jnp.stack(jnp.split(wide_band, lax.axis_size("past"), axis=1)), "past", 0, 0
+        ),
+        axis=0,
+    )
     orbitals = pair_coupling.shape[0]
     memory_next = (
         memory[1].astype(jnp.float32) + orbital_flip(gathered, orbitals).astype(jnp.float32)

time: 303 us -> 297 us (0.980)
  local copies, waits for them, and re-layouts: 86.1 us -> 83 us
where the time goes in v1:
time: 297 us; the launch traced here: 296 us
  waiting for transfers between devices  130 us (44%)
  local copies, waits for them, and re-layouts  83 us (28%)
  matrix products  34.2 us (12%)
  blocking collectives  32 us (11%)
  between operations  13.2 us (4%)
  other arithmetic  3.95 us (1%)
    psum x2, waiting for transfers between devices, advance(): lax.psum(partial_value.astype(jnp.bfloat16), 'past').astype(jnp.float32)  98.1 us
    convert_element_type x3, local copies, waits for them, and re-layouts, per_device(): orbital_flip(gathered, orbitals).astype(jnp.float32)  46.4 us
    all_to_all x1, blocking collectives, per_device(): lax.all_to_all(jnp.stack(jnp.split(wide_band, lax.axis_size('past'), axis...  32 us
    all_gather x1, waiting for transfers between devices, per_device(): wide_band = lax.all_gather(own_rows, 'second', axis=1, tiled=True)  31.5 us
    dot_general x2, matrix products, advance(): jnp.dot(memory_row, resident, preferred_element_type=jnp.float32)  19.9 us
    dot_general x2, matrix products, solve_front(): jnp.dot(inverse_block, source, precision=lax.Precision.HIGHEST, preferred...  14.3 us
    mul x2, local copies, waits for them, and re-layouts, self_energy(): blocks * pair_coupling[None, :, None, :]  11.3 us
    transpose x1, local copies, waits for them, and re-layouts, orbital_flip(): return blocks.transpose(0, 3, 2, 1).reshape(row_count, col_count)  10.8 us
  transfers between devices with their start and end apart: 3, of which 3 were waited for; matrix products, arithmetic and copies ran while one was open for 4% of the time, Pallas kernels for 0%

profile of v1, /device:TPU:0, one launch (start us, length us, event | category | flops | bytes accessed | tf_op | source)
XLA Modules:
  0.0 296.2 jit_solution(16054703843870884580)
XLA Ops:
  6.5 9.2 %convolution_convert_fusion.1 = bf16[384,1536]{1,0:T(8,128)(2,1)} fusion(bf16[3072,1536]{1,0:T(8,128)(2,1)} %param.5, bf16[2,384,3072]{2,1,0:T(8,128)(2,1)} %param.6), kind=kOutput, calls=%fused_computation.9 | convolution fusion | flops 3624468480 | bytes 12976128 | tf_op jit(solution)/shard_map/dot_general | solution.py:42
  15.8 0.0 all-reduce.3.cloned.1.call-update
  15.8 0.0 all-gather.2.cloned.1.call-start
  15.9 4.4 %mul.29 = f32[12,32,48,32]{3,2,1,0:T(8,128)} broadcast(f32[32,32]{1,0:T(8,128)S(1)} %copy-done), dimensions={1,3} | broadcast | bytes 2363392 | tf_op jit(solution)/shard_map/mul | solution.py:32
  20.3 6.9 %mul.30 = f32[384,1536]{1,0:T(8,128)S(1)} reshape(f32[12,32,48,32]{3,2,1,0:T(8,128)} %mul.29) | data formatting | bytes 4718592 | tf_op jit(solution)/shard_map/mul | solution.py:32
  27.2 45.8 %all-reduce.3.cloned.1.call-done = bf16[384,1536]{1,0:T(8,128)(2,1)} async-done(((bf16[384,1536]{1,0:T(8,128)(2,1)}), bf16[384,1536]{1,0:T(8,128)(2,1)}) %all-reduce.3.cloned.1.call-update) | async-done | bytes 1179664 | tf_op jit(solution)/shard_map/psum | solution.py:43
  73.0 8.2 %fusion.28 = (f32[384,1536]{1,0:T(8,128)}, bf16[384,1536]{1,0:T(8,128)(2,1)S(1)}) fusion(f32[2,384,384]{2,1,0:T(8,128)} %param.8, bf16[384,1536]{1,0:T(8,128)(2,1)} %all-reduce.3.cloned.1.call-done, bf16[2,384,1536]{2,1,0:T(8,128)(2,1)} %param.7), kind=kOutput, calls=%fused_computation.43 | convolution fusion | flops 2724397056 | bytes 8847360 | tf_op jit(solution)/shard_map/dot_general | solution.py:17
  81.2 5.0 %reshape.21 = f32[12,32,48,32]{3,2,1,0:T(8,128)} reshape(bf16[384,1536]{1,0:T(8,128)(2,1)S(1)} %get-tuple-element.10) | data formatting | bytes 3538944 | tf_op jit(solution)/shard_map/reshape | solution.py:11
  86.2 10.8 %copy.9 = f32[12,32,48,32]{3,2,1,0:T(8,128)} copy(f32[12,32,48,32]{1,2,3,0:T(8,128)} %bitcast.67) | data formatting | bytes 4718592 | tf_op jit(solution)/shard_map/transpose | solution.py:12
  97.0 7.7 %reshape.22 = f32[384,1536]{1,0:T(8,128)} reshape(f32[12,32,48,32]{3,2,1,0:T(8,128)} %copy.9) | data formatting | bytes 4718592 | tf_op jit(solution)/shard_map/reshape | solution.py:12
  104.8 2.0 fusion.21
  106.8 0.0 all-gather.2.cloned.1.call-update
  106.8 0.0 all-reduce.5.cloned.1.call-start
  106.9 31.5 %all-gather.2.cloned.1.call-done = bf16[96,12288]{1,0:T(8,128)(2,1)} async-done(((bf16[96,1536]{1,0:T(8,128)(2,1)}), bf16[96,12288]{1,0:T(8,128)(2,1)}) %all-gather.2.cloned.1.call-update) | async-done | bytes 2359312 | tf_op jit(solution)/shard_map/all_gather | solution.py:51
  138.4 1.8 slice_bitcast_fusion.3
  140.2 0.3 pad_maximum_fusion
  140.5 32.0 %all_to_all.5 = bf16[4,96,3072]{2,1,0:T(8,128)(2,1)S(1)} all-to-all(bf16[4,96,3072]{2,1,0:T(8,128)(2,1)S(1)} %pad_maximum_fusion), channel_id=1, replica_groups=mesh['past'=4,'second'=8] {'past'}, dimensions={0} | all-to-all | bytes 4718592 | tf_op jit(solution)/shard_map/all_to_all | solution.py:53
  172.5 9.4 %reshape.27 = f32[12,32,96,32]{3,2,1,0:T(8,128)} reshape(bf16[4,96,3072]{2,1,0:T(8,128)(2,1)S(1)} %all_to_all.5) | data formatting | bytes 7077888 | tf_op jit(solution)/shard_map/convert_element_type | solution.py:60
  181.9 22.5 %copy.10 = f32[12,32,96,32]{3,2,1,0:T(8,128)} copy(f32[12,32,96,32]{1,2,3,0:T(8,128)} %bitcast.66) | data formatting | bytes 9437184 | tf_op jit(solution)/shard_map/convert_element_type | solution.py:60
  204.4 14.6 %reshape.26 = f32[384,3072]{1,0:T(8,128)} reshape(f32[12,32,96,32]{3,2,1,0:T(8,128)} %copy.10) | data formatting | bytes 9437184 | tf_op jit(solution)/shard_map/convert_element_type | solution.py:60
  218.9 10.7 %convolution_convert_fusion = bf16[384,1536]{1,0:T(8,128)(2,1)} fusion(bf16[3072,1536]{1,0:T(8,128)(2,1)} %param.5, f32[384,3072]{1,0:T(8,128)} %reshape.26, bf16[2,384,3072]{2,1,0:T(8,128)(2,1)} %param.6), kind=kOutput, calls=%fused_computation.8 | convolution fusion | flops 3628007424 | bytes 17694720 | tf_op jit(solution)/shard_map/dot_general | solution.py:42
  229.7 52.3 %all-reduce.5.cloned.1.call-done = bf16[384,1536]{1,0:T(8,128)(2,1)} async-done(((bf16[384,1536]{1,0:T(8,128)(2,1)}), bf16[384,1536]{1,0:T(8,128)(2,1)}) %all-reduce.5.cloned.1.call-update) | async-done | bytes 1179664 | tf_op jit(solution)/shard_map/psum | solution.py:43
  282.0 6.1 %fusion.5 = bf16[1,384,1536]{2,1,0:T(8,128)(2,1)S(1)} fusion(bf16[384,1536]{1,0:T(8,128)(2,1)} %all-reduce.5.cloned.1.call-done, bf16[2,384,1536]{2,1,0:T(8,128)(2,1)S(1)} %copy-done.1, f32[2,384,384]{2,1,0:T(8,128)} %param.8), kind=kOutput, calls=%fused_computation.10 | convolution fusion | flops 2723807232 | bytes 6488064 | tf_op jit(solution)/shard_map/dot_general | solution.py:17
  288.0 1.6 pad_maximum_fusion.1
  (6 shorter events, 0.0 us)
Async XLA Ops:
  6.5 9.3 %copy-start = (f32[32,32]{1,0:T(8,128)S(1)}, f32[32,32]{1,0:T(8,128)}, u32[]{:S(2)}) copy-start(f32[32,32]{1,0:T(8,128)} %param.9) | copy-start | bytes 12292
  6.5 66.5 %all-reduce.3.cloned.1.call-start = ((), (), s32[]{:S(2)}) async-start(), calls=%async_computation.1 | async-start | bytes 2359296 | tf_op jit(solution)/shard_map/psum | solution.py:43
  15.8 122.6 %all-gather.2.cloned.1.call-start = ((), (), s32[]{:S(2)}) async-start(), calls=%async_computation.2 | async-start | bytes 2654208 | tf_op jit(solution)/shard_map/all_gather | solution.py:51
  106.8 175.1 %all-reduce.5.cloned.1.call-start = ((), (), s32[]{:S(2)}) async-start(), calls=%async_computation.3 | async-start | bytes 2359296 | tf_op jit(solution)/shard_map/psum | solution.py:43
  218.9 63.0 %copy-start.1 = (bf16[2,384,1536]{2,1,0:T(8,128)(2,1)S(1)}, bf16[2,384,1536]{2,1,0:T(8,128)(2,1)}, u32[]{:S(2)}) copy-start(bf16[2,384,1536]{2,1,0:T(8,128)(2,1)} %param.7) | copy-start | bytes 7077892
Sparse Core Ops, SparseCore 0:
  15.9 57.0 all-reduce.2
  106.9 31.4 all-gather.1
  229.8 52.1 all-reduce.4
